TPU v7x, 512 devices: a whole 4x4x16 slice. The times are simulated.
512 devices in a mesh: pts: 16 (over z), elem: 32 (over y, x, core).
Axes of the slice: x: 4, y: 4, z: 16, core: 2. Of those that a mesh axis runs over, the one named last changes fastest.
Arguments:
- theta: float32 [1024, 1024], P('elem', 'pts'), may hold values from -3.140625 to 3.140625
- panel_rows: int32 [1024], P('elem'), may hold values from 0 to 1023, each once
- point_rows: int32 [32768], P('pts'), may hold values from 0 to 511
- point_cols: int32 [32768], P('pts'), may hold values from 0 to 255
- direct: float32 [2, 32768], P(None, 'pts'), may hold values from -3 to 3
- noise: float32 [32768], P('pts'), may hold values from 0.05 to 0.5
Outputs:
- phase_grad: float32 [1024, 1024], P('elem', 'pts')
- field: float32 [2, 32768], P(None, 'pts')
Inputs may be any that keep to these rules, and one draw needn't show every extreme that they name: `panel_rows`: each lattice row appears once.
All inputs are finite; a program needn't handle non-finite values.
Results may differ from a plain program's by a relative error of at most 0.0004.
Values sent between devices are 32-bit elements; how exact they have to be, the bound alone decides.
No kernel may reach another device: no remote copies, remote signals or barrier semaphores. Data moves between devices by JAX's collectives and lax.ppermute only.
A program may use at most 64 MiB of HBM per device.

v0:
```python
import math
import jax
import jax.numpy as jnp
from jax import lax
from jax.sharding import PartitionSpec as P

NX_EL = 1024
NY_EL = 1024
HIGH = lax.Precision.HIGHEST


def geometry(point_rows, point_cols):
    along_x = (point_rows.astype(jnp.float32) - 255.5) * 0.5
    along_y = (point_cols.astype(jnp.float32) - 127.5) * 0.5
    radius = jnp.sqrt(along_x * along_x + along_y * along_y + 1600.0)
    return (along_x / radius, along_y / radius, 80.0 / (radius * math.sqrt(NX_EL * NY_EL)))


def partial_field(slope_x, slope_y, lattice_x, lattice_y, phase_re, phase_im):
    beam_y = math.pi * slope_y[:, None] * lattice_y[None, :]
    left = jnp.concatenate([jnp.cos(beam_y), jnp.sin(beam_y)], 1)
    right = jnp.concatenate(
        [
            jnp.concatenate([phase_re.T, phase_im.T], 1),
            jnp.concatenate([-phase_im.T, phase_re.T], 1),
        ],
        0,
    )
    inner = jnp.dot(left, right, precision=HIGH, preferred_element_type=jnp.float32)
    width = phase_re.shape[0]
    inner_re = inner[:, :width]
    inner_im = inner[:, width:]
    beam_x = math.pi * slope_x[:, None] * lattice_x[None, :]
    cos_x = jnp.cos(beam_x)
    sin_x = jnp.sin(beam_x)
    return jnp.stack(
        [
            jnp.sum(cos_x * inner_re - sin_x * inner_im, 1),
            jnp.sum(cos_x * inner_im + sin_x * inner_re, 1),
        ]
    )


def surface_terms(slope_x, slope_y, q_re, q_im, lattice_x, lattice_y):
    beam_x = math.pi * slope_x[:, None] * lattice_x[None, :]
    cos_x = jnp.cos(beam_x)
    sin_x = jnp.sin(beam_x)
    weight_re = q_re[:, None] * cos_x - q_im[:, None] * sin_x
    weight_im = q_re[:, None] * sin_x + q_im[:, None] * cos_x
    beam_y = math.pi * slope_y[:, None] * lattice_y[None, :]
    left = jnp.concatenate([jnp.cos(beam_y), jnp.sin(beam_y)], 1)
    right = jnp.concatenate([weight_re, weight_im], 1)
    prod = lax.dot_general(
        left, right, (((0,), (0,)), ((), ())), precision=HIGH, preferred_element_type=jnp.float32
    )
    rows_y = lattice_y.shape[0]
    cols_x = lattice_x.shape[0]
    sum_re = prod[:rows_y, :cols_x] - prod[rows_y:, cols_x:]
    sum_im = prod[:rows_y, cols_x:] + prod[rows_y:, :cols_x]
    return jnp.concatenate([sum_re, sum_im], 1)


def block_size(points, cols_y):
    return math.gcd(points, min(points, max(256, 524288 // cols_y)))


def field_blocks(slope_x, slope_y, lattice_x, lattice_y, phase_re, phase_im):
    block = block_size(slope_x.shape[0], lattice_y.shape[0])
    count = slope_x.shape[0] // block

    def one_block(pair):
        return partial_field(pair[0], pair[1], lattice_x, lattice_y, phase_re, phase_im)

    parts = lax.map(one_block, (slope_x.reshape(count, block), slope_y.reshape(count, block)))
    return jnp.transpose(parts, (1, 0, 2)).reshape(2, count * block)


def terms_blocks(slope_x, slope_y, q_re, q_im, lattice_x, lattice_y):
    block = block_size(slope_x.shape[0], lattice_y.shape[0])
    count = slope_x.shape[0] // block
    start = jnp.zeros((lattice_y.shape[0], 2 * lattice_x.shape[0]), jnp.float32)

    def step(carry, items):
        return (
            carry + surface_terms(items[0], items[1], items[2], items[3], lattice_x, lattice_y),
            None,
        )

    items = (
        slope_x.reshape(count, block),
        slope_y.reshape(count, block),
        q_re.reshape(count, block),
        q_im.reshape(count, block),
    )
    total, unused = lax.scan(step, start, items)
    return total


def weights(field, scale, noise):
    power = noise + field[0] * field[0] + field[1] * field[1]
    return (field[0] * scale / power, -field[1] * scale / power)


def gradient(terms, phase_re, phase_im):
    cols_x = phase_re.shape[0]
    sum_re = terms[:, :cols_x].T
    sum_im = terms[:, cols_x:].T
    return -2.0 * (phase_re * sum_im + phase_im * sum_re)


def shards(theta, panel_rows, point_rows, point_cols, direct, noise):
    slope_x, slope_y, scale = geometry(point_rows, point_cols)
    phase_re = jnp.cos(theta)
    phase_im = jnp.sin(theta)
    lattice_x = panel_rows.astype(jnp.float32) - (NX_EL - 1) / 2.0
    cols_dev = theta.shape[1]
    phasors = jnp.stack([phase_re, phase_im])
    whole = lax.all_gather(phasors, "pts", axis=2, tiled=True)
    lattice_y = jnp.arange(NY_EL).astype(jnp.float32) - (NY_EL - 1) / 2.0
    partial_value = field_blocks(slope_x, slope_y, lattice_x, lattice_y, whole[0], whole[1])
    total = lax.psum(partial_value, "elem")
    field = direct + scale[None, :] * total
    q_re, q_im = weights(field, scale, noise)
    cols_here = jnp.arange(cols_dev * lax.axis_size("pts")).astype(jnp.float32) - (NY_EL - 1) / 2.0
    terms = lax.psum_scatter(
        terms_blocks(slope_x, slope_y, q_re, q_im, lattice_x, cols_here),
        "pts",
        scatter_dimension=0,
        tiled=True,
    )
    return (gradient(terms, phase_re, phase_im), field)


def solution(mesh):
    in_specs = (P("elem", "pts"), P("elem"), P("pts"), P("pts"), P(None, "pts"), P("pts"))
    out_specs = (P("elem", "pts"), P(None, "pts"))
    return jax.shard_map(shards, mesh=mesh, in_specs=in_specs, out_specs=out_specs, check_vma=False)
```

profile of v0, /device:TPU:2, one launch (start us, length us, event | category | flops | bytes accessed | tf_op | source)
XLA Modules:
  0.0 337.5 jit_solution(4195258781509086454)
XLA Ops:
  8.3 41.7 %all_gather.3 = f32[2,32,1024]{1,0,2:T(2,128)S(1)} all-gather(f32[2,32,64]{1,0,2:T(2,128)S(1)} %pad_maximum_fusion), channel_id=1, replica_groups=mesh['pts'=16,'elem'=32] {'pts'}, dimensions={2}, use_global_device_ids=true | all-gather | bytes 278528 | tf_op jit(solution)/shard_map/all_gather | solution.py:118
  49.9 0.8 fusion.38
  51.3 47.9 %while.24 = (s32[]{:T(128)}, f32[4,2,512]{2,1,0:T(2,128)S(1)}, f32[4,512]{1,0:T(4,128)S(1)}, f32[32]{0:T(128)S(1)}, f32[4,512]{1,0:T(4,128)S(1)}, /*index=5*/f32[2048,64]{1,0:T(8,128)S(1)}, s32[]{:T(128)}) while((s32[]{:T(128)}, f32[4,2,512]{2,1,0:T(2,128)S(1)}, f32[4,512]{1,0:T(4,128)S(1)}, f32[32]{0:T(128)S(1)}, ...), condition=%wide.region_3.4_spmd.clone, body=%wide.region_0.3_spmd.clone.sunk | while | flops 807029760 | bytes 9208021 | solution.py:74
  51.3 7.3 %multiply_cosine_fusion.6 = (f32[512,1024]{1,0:T(8,128)S(1)}, f32[512,1024]{1,0:T(8,128)S(1)}) fusion(f32[1024]{0:T(1024)S(1)} %convert_add_fusion.5, f32[512]{0:T(512)S(1)} %bitcast.76), kind=kLoop, calls=%fused_computation.7.clone.1 | loop fusion | flops 524288 | bytes 4200448 | tf_op jit(solution)/shard_map/while/body/eval_jaxpr/cos | solution.py:21
  58.7 4.2 %fusion.52 = f32[512,64]{0,1:T(8,128)S(1)} fusion(f32[2048,64]{1,0:T(8,128)S(1)} %get-tuple-element.375, f32[512,1024]{1,0:T(8,128)S(1)} %get-tuple-element.334, f32[512,1024]{1,0:T(8,128)S(1)} %get-tuple-element.335), kind=kOutput, calls=%fused_computation.2.clone.1 | convolution fusion | flops 806354944 | bytes 4849664 | tf_op jit(solution)/shard_map/while/body/eval_jaxpr/dot_general | solution.py:29
  63.3 7.3 %multiply_cosine_fusion.6 = (f32[512,1024]{1,0:T(8,128)S(1)}, f32[512,1024]{1,0:T(8,128)S(1)}) fusion(f32[1024]{0:T(1024)S(1)} %convert_add_fusion.5, f32[512]{0:T(512)S(1)} %bitcast.76), kind=kLoop, calls=%fused_computation.7.clone.1 | loop fusion | flops 524288 | bytes 4200448 | tf_op jit(solution)/shard_map/while/body/eval_jaxpr/cos | solution.py:21
  70.6 4.2 %fusion.52 = f32[512,64]{0,1:T(8,128)S(1)} fusion(f32[2048,64]{1,0:T(8,128)S(1)} %get-tuple-element.375, f32[512,1024]{1,0:T(8,128)S(1)} %get-tuple-element.334, f32[512,1024]{1,0:T(8,128)S(1)} %get-tuple-element.335), kind=kOutput, calls=%fused_computation.2.clone.1 | convolution fusion | flops 806354944 | bytes 4849664 | tf_op jit(solution)/shard_map/while/body/eval_jaxpr/dot_general | solution.py:29
  75.3 7.3 %multiply_cosine_fusion.6 = (f32[512,1024]{1,0:T(8,128)S(1)}, f32[512,1024]{1,0:T(8,128)S(1)}) fusion(f32[1024]{0:T(1024)S(1)} %convert_add_fusion.5, f32[512]{0:T(512)S(1)} %bitcast.76), kind=kLoop, calls=%fused_computation.7.clone.1 | loop fusion | flops 524288 | bytes 4200448 | tf_op jit(solution)/shard_map/while/body/eval_jaxpr/cos | solution.py:21
  82.6 4.2 %fusion.52 = f32[512,64]{0,1:T(8,128)S(1)} fusion(f32[2048,64]{1,0:T(8,128)S(1)} %get-tuple-element.375, f32[512,1024]{1,0:T(8,128)S(1)} %get-tuple-element.334, f32[512,1024]{1,0:T(8,128)S(1)} %get-tuple-element.335), kind=kOutput, calls=%fused_computation.2.clone.1 | convolution fusion | flops 806354944 | bytes 4849664 | tf_op jit(solution)/shard_map/while/body/eval_jaxpr/dot_general | solution.py:29
  87.2 7.3 %multiply_cosine_fusion.6 = (f32[512,1024]{1,0:T(8,128)S(1)}, f32[512,1024]{1,0:T(8,128)S(1)}) fusion(f32[1024]{0:T(1024)S(1)} %convert_add_fusion.5, f32[512]{0:T(512)S(1)} %bitcast.76), kind=kLoop, calls=%fused_computation.7.clone.1 | loop fusion | flops 524288 | bytes 4200448 | tf_op jit(solution)/shard_map/while/body/eval_jaxpr/cos | solution.py:21
  94.6 4.2 %fusion.52 = f32[512,64]{0,1:T(8,128)S(1)} fusion(f32[2048,64]{1,0:T(8,128)S(1)} %get-tuple-element.375, f32[512,1024]{1,0:T(8,128)S(1)} %get-tuple-element.334, f32[512,1024]{1,0:T(8,128)S(1)} %get-tuple-element.335), kind=kOutput, calls=%fused_computation.2.clone.1 | convolution fusion | flops 806354944 | bytes 4849664 | tf_op jit(solution)/shard_map/while/body/eval_jaxpr/dot_general | solution.py:29
  99.2 119.2 %psum.7 = f32[2,2048]{1,0:T(2,128)S(1)} all-reduce(f32[2,2048]{1,0:T(2,128)S(1)} %bitcast.82), channel_id=1, replica_groups=mesh['pts'=16,'elem'=32] {'elem'}, use_global_device_ids=true, to_apply=%region_4.5 | all-reduce | flops 4096 | bytes 32768 | tf_op jit(solution)/shard_map/psum | solution.py:121
  219.0 42.9 %while.25 = (s32[]{:T(128)}, f32[1024,64]{0,1:T(8,128)S(1)}, f32[4,512]{1,0:T(4,128)S(1)}, f32[4,512]{1,0:T(4,128)S(1)}, f32[4,512]{1,0:T(4,128)S(1)}, /*index=5...) while((s32[]{:T(128)}, f32[1024,64]{0,1:T(8,128)S(1)}, f32[4,512]{1,0:T(4,128)S(1)}, ...), condition=%wide.region_6.7_spmd.clone, body=%wide.region_5.6_spmd.clone.sunk | while | flops 807291904 | bytes 10780911 | solution.py:95
  219.3 7.3 %multiply_cosine_fusion.7 = (f32[512,1024]{1,0:T(8,128)S(1)}, f32[512,1024]{1,0:T(8,128)S(1)}) fusion(f32[1024]{0:T(1024)S(1)} %convert_add_fusion.6, f32[512]{0:T(512)S(1)} %bitcast.72), kind=kLoop, calls=%fused_computation.29.clone.1 | loop fusion | flops 524288 | bytes 4200448 | tf_op jit(solution)/shard_map/while/body/eval_jaxpr/cos | solution.py:51
  226.7 2.8 fusion.58
  230.1 7.3 %multiply_cosine_fusion.7 = (f32[512,1024]{1,0:T(8,128)S(1)}, f32[512,1024]{1,0:T(8,128)S(1)}) fusion(f32[1024]{0:T(1024)S(1)} %convert_add_fusion.6, f32[512]{0:T(512)S(1)} %bitcast.72), kind=kLoop, calls=%fused_computation.29.clone.1 | loop fusion | flops 524288 | bytes 4200448 | tf_op jit(solution)/shard_map/while/body/eval_jaxpr/cos | solution.py:51
  237.4 2.8 fusion.58
  240.8 7.3 %multiply_cosine_fusion.7 = (f32[512,1024]{1,0:T(8,128)S(1)}, f32[512,1024]{1,0:T(8,128)S(1)}) fusion(f32[1024]{0:T(1024)S(1)} %convert_add_fusion.6, f32[512]{0:T(512)S(1)} %bitcast.72), kind=kLoop, calls=%fused_computation.29.clone.1 | loop fusion | flops 524288 | bytes 4200448 | tf_op jit(solution)/shard_map/while/body/eval_jaxpr/cos | solution.py:51
  248.1 2.8 fusion.58
  251.5 7.3 %multiply_cosine_fusion.7 = (f32[512,1024]{1,0:T(8,128)S(1)}, f32[512,1024]{1,0:T(8,128)S(1)}) fusion(f32[1024]{0:T(1024)S(1)} %convert_add_fusion.6, f32[512]{0:T(512)S(1)} %bitcast.72), kind=kLoop, calls=%fused_computation.29.clone.1 | loop fusion | flops 524288 | bytes 4200448 | tf_op jit(solution)/shard_map/while/body/eval_jaxpr/cos | solution.py:51
  258.8 2.8 fusion.58
  261.8 1.0 copy.26
  262.9 66.2 %reduce-scatter.4.cloned.1.call-done = f32[64,64]{1,0:T(8,128)} async-done(((f32[1024,64]{1,0:T(8,128)}), f32[64,64]{1,0:T(8,128)}) %reduce-scatter.4.cloned.1.call-update) | async-done | bytes 16400 | tf_op jit(solution)/shard_map/reduce_scatter | solution.py:125
  329.1 0.9 fusion.34
  (71 shorter events, 6.1 us)
Async XLA Ops:
  7.2 321.9 %reduce-scatter.4.cloned.1.call-start = ((), (), s32[]{:S(2)}) async-start(), calls=%async_computation.1 | async-start | bytes 557056 | tf_op jit(solution)/shard_map/reduce_scatter | solution.py:125
  8.2 42.6 %copy-start.2 = (s32[2048]{0:T(1024)S(1)}, s32[2048]{0:T(1024)}, u32[]{:S(2)}) copy-start(s32[2048]{0:T(1024)} %param.13) | copy-start | bytes 24580
  8.3 42.6 %copy-start.3 = (s32[2048]{0:T(1024)S(1)}, s32[2048]{0:T(1024)}, u32[]{:S(2)}) copy-start(s32[2048]{0:T(1024)} %param.12) | copy-start | bytes 24580
  8.3 42.6 %copy-start.5 = (s32[32]{0:T(128)S(1)}, s32[32]{0:T(128)}, u32[]{:S(2)}) copy-start(s32[32]{0:T(128)} %param.11) | copy-start | bytes 388
  51.2 167.1 %copy-start.1 = (f32[2,2048]{1,0:T(2,128)S(1)}, f32[2,2048]{1,0:T(2,128)}, u32[]{:S(2)}) copy-start(f32[2,2048]{1,0:T(2,128)} %param.14) | copy-start | bytes 49156
  51.3 167.1 %copy-start.4 = (f32[2048]{0:T(1024)S(1)}, f32[2048]{0:T(1024)}, u32[]{:S(2)}) copy-start(f32[2048]{0:T(1024)} %param.15) | copy-start | bytes 24580
  218.4 0.6 copy-start
Sparse Core Ops, SparseCore 0:
  263.0 66.0 reduce-scatter.3
where the time goes:
time: 338 us
  blocking collectives  161 us (48%)
  waiting for transfers between devices  66.2 us (20%)
  other arithmetic  63.5 us (19%)
  matrix products  28.3 us (8%)
  between operations  14.2 us (4%)
  local copies, waits for them, and re-layouts  4.05 us (1%)
    psum x1, blocking collectives, shards(): total = lax.psum(partial_value, 'elem')  119 us
    reduce_scatter x1, waiting for transfers between devices, shards(): lax.psum_scatter(terms_blocks(slope_x, slope_y, q_re, q_im, lattice_x, co...  66.2 us
    all_gather x1, blocking collectives, shards(): whole = lax.all_gather(phasors, 'pts', axis=2, tiled=True)  41.7 us
    cos x4, other arithmetic, partial_field(): left = jnp.concatenate([jnp.cos(beam_y), jnp.sin(beam_y)], 1)  29.4 us
    cos x4, other arithmetic, surface_terms(): left = jnp.concatenate([jnp.cos(beam_y), jnp.sin(beam_y)], 1)  29.4 us
    dot_general x4, matrix products, partial_field(): jnp.dot(left, right, precision=HIGH, preferred_element_type=jnp.float32)  16.9 us
    dot_general x4, matrix products, surface_terms(): lax.dot_general(left, right, (((0,), (0,)), ((), ())), precision=HIGH, pr...  11.4 us
  transfers between devices with their start and end apart: 1, of which 1 were waited for; matrix products, arithmetic and copies ran while one was open for 0% of the time, Pallas kernels for 0%

commit v1 on v0

--- a/solution.py
+++ b/solution.py
@@ -1,3 +1,4 @@
+import functools
 import math
 import jax
 import jax.numpy as jnp
@@ -7,6 +8,13 @@
 NX_EL = 1024
 NY_EL = 1024
 HIGH = lax.Precision.HIGHEST
+
+
+def _arrange_regions(shard_in, bus_axis):
+    return lax.all_gather(shard_in, axis_name=bus_axis).sum(axis=0)
+
+
+report_knots = functools.partial(_arrange_regions, bus_axis="elem")
 
 
 def geometry(point_rows, point_cols):
@@ -118,7 +126,7 @@
     whole = lax.all_gather(phasors, "pts", axis=2, tiled=True)
     lattice_y = jnp.arange(NY_EL).astype(jnp.float32) - (NY_EL - 1) / 2.0
     partial_value = field_blocks(slope_x, slope_y, lattice_x, lattice_y, whole[0], whole[1])
-    total = lax.psum(partial_value, "elem")
+    total = report_knots(partial_value)
     field = direct + scale[None, :] * total
     q_re, q_im = weights(field, scale, noise)
     cols_here = jnp.arange(cols_dev * lax.axis_size("pts")).astype(jnp.float32) - (NY_EL - 1) / 2.0

time: 338 us -> 242 us (0.72)
  the two profiles are of different devices: /device:TPU:2 before, /device:TPU:4 now
where the time goes in v1:
time: 242 us
  blocking collectives  66.6 us (28%)
  waiting for transfers between devices  64.5 us (27%)
  other arithmetic  63.7 us (26%)
  matrix products  28.3 us (12%)
  between operations  14.2 us (6%)
  local copies, waits for them, and re-layouts  4.05 us (2%)
    reduce_scatter x1, waiting for transfers between devices, shards(): lax.psum_scatter(terms_blocks(slope_x, slope_y, q_re, q_im, lattice_x, co...  64.5 us
    all_gather x1, blocking collectives, shards(): whole = lax.all_gather(phasors, 'pts', axis=2, tiled=True)  41.7 us
    cos x4, other arithmetic, partial_field(): left = jnp.concatenate([jnp.cos(beam_y), jnp.sin(beam_y)], 1)  29.4 us
    cos x4, other arithmetic, surface_terms(): left = jnp.concatenate([jnp.cos(beam_y), jnp.sin(beam_y)], 1)  29.4 us
    all_gather x1, blocking collectives, _arrange_regions(): return lax.all_gather(shard_in, axis_name=bus_axis).sum(axis=0)  24.9 us
    dot_general x4, matrix products, partial_field(): jnp.dot(left, right, precision=HIGH, preferred_element_type=jnp.float32)  16.9 us
    dot_general x4, matrix products, surface_terms(): lax.dot_general(left, right, (((0,), (0,)), ((), ())), precision=HIGH, pr...  11.4 us
  transfers between devices with their start and end apart: 1, of which 1 were waited for; matrix products, arithmetic and copies ran while one was open for 0% of the time, Pallas kernels for 0%

profile of v1, /device:TPU:4, one launch (start us, length us, event | category | flops | bytes accessed | tf_op | source)
XLA Modules:
  0.0 241.8 jit_solution(1602336793773625345)
XLA Ops:
  8.3 41.7 %all_gather.6 = f32[2,32,1024]{1,0,2:T(2,128)S(1)} all-gather(f32[2,32,64]{1,0,2:T(2,128)S(1)} %pad_maximum_fusion), channel_id=1, replica_groups=mesh['pts'=16,'elem'=32] {'pts'}, dimensions={2}, use_global_device_ids=true | all-gather | bytes 278528 | tf_op jit(solution)/shard_map/all_gather | solution.py:126
  49.9 0.8 fusion.38
  51.3 47.9 %while.24 = (s32[]{:T(128)}, f32[4,2,512]{2,1,0:T(2,128)S(1)}, f32[4,512]{1,0:T(4,128)S(1)}, f32[32]{0:T(128)S(1)}, f32[4,512]{1,0:T(4,128)S(1)}, /*index=5*/f32[2048,64]{1,0:T(8,128)S(1)}, s32[]{:T(128)}) while((s32[]{:T(128)}, f32[4,2,512]{2,1,0:T(2,128)S(1)}, f32[4,512]{1,0:T(4,128)S(1)}, f32[32]{0:T(128)S(1)}, ...), condition=%wide.region_3.4_spmd.clone, body=%wide.region_0.3_spmd.clone.sunk | while | flops 807029760 | bytes 9208021 | solution.py:82
  51.3 7.3 %multiply_cosine_fusion.6 = (f32[512,1024]{1,0:T(8,128)S(1)}, f32[512,1024]{1,0:T(8,128)S(1)}) fusion(f32[1024]{0:T(1024)S(1)} %convert_add_fusion.5, f32[512]{0:T(512)S(1)} %bitcast.76), kind=kLoop, calls=%fused_computation.7.clone.1 | loop fusion | flops 524288 | bytes 4200448 | tf_op jit(solution)/shard_map/while/body/eval_jaxpr/cos | solution.py:29
  58.7 4.2 %fusion.52 = f32[512,64]{0,1:T(8,128)S(1)} fusion(f32[2048,64]{1,0:T(8,128)S(1)} %get-tuple-element.375, f32[512,1024]{1,0:T(8,128)S(1)} %get-tuple-element.334, f32[512,1024]{1,0:T(8,128)S(1)} %get-tuple-element.335), kind=kOutput, calls=%fused_computation.2.clone.1 | convolution fusion | flops 806354944 | bytes 4849664 | tf_op jit(solution)/shard_map/while/body/eval_jaxpr/dot_general | solution.py:37
  63.3 7.3 %multiply_cosine_fusion.6 = (f32[512,1024]{1,0:T(8,128)S(1)}, f32[512,1024]{1,0:T(8,128)S(1)}) fusion(f32[1024]{0:T(1024)S(1)} %convert_add_fusion.5, f32[512]{0:T(512)S(1)} %bitcast.76), kind=kLoop, calls=%fused_computation.7.clone.1 | loop fusion | flops 524288 | bytes 4200448 | tf_op jit(solution)/shard_map/while/body/eval_jaxpr/cos | solution.py:29
  70.6 4.2 %fusion.52 = f32[512,64]{0,1:T(8,128)S(1)} fusion(f32[2048,64]{1,0:T(8,128)S(1)} %get-tuple-element.375, f32[512,1024]{1,0:T(8,128)S(1)} %get-tuple-element.334, f32[512,1024]{1,0:T(8,128)S(1)} %get-tuple-element.335), kind=kOutput, calls=%fused_computation.2.clone.1 | convolution fusion | flops 806354944 | bytes 4849664 | tf_op jit(solution)/shard_map/while/body/eval_jaxpr/dot_general | solution.py:37
  75.3 7.3 %multiply_cosine_fusion.6 = (f32[512,1024]{1,0:T(8,128)S(1)}, f32[512,1024]{1,0:T(8,128)S(1)}) fusion(f32[1024]{0:T(1024)S(1)} %convert_add_fusion.5, f32[512]{0:T(512)S(1)} %bitcast.76), kind=kLoop, calls=%fused_computation.7.clone.1 | loop fusion | flops 524288 | bytes 4200448 | tf_op jit(solution)/shard_map/while/body/eval_jaxpr/cos | solution.py:29
  82.6 4.2 %fusion.52 = f32[512,64]{0,1:T(8,128)S(1)} fusion(f32[2048,64]{1,0:T(8,128)S(1)} %get-tuple-element.375, f32[512,1024]{1,0:T(8,128)S(1)} %get-tuple-element.334, f32[512,1024]{1,0:T(8,128)S(1)} %get-tuple-element.335), kind=kOutput, calls=%fused_computation.2.clone.1 | convolution fusion | flops 806354944 | bytes 4849664 | tf_op jit(solution)/shard_map/while/body/eval_jaxpr/dot_general | solution.py:37
  87.2 7.3 %multiply_cosine_fusion.6 = (f32[512,1024]{1,0:T(8,128)S(1)}, f32[512,1024]{1,0:T(8,128)S(1)}) fusion(f32[1024]{0:T(1024)S(1)} %convert_add_fusion.5, f32[512]{0:T(512)S(1)} %bitcast.76), kind=kLoop, calls=%fused_computation.7.clone.1 | loop fusion | flops 524288 | bytes 4200448 | tf_op jit(solution)/shard_map/while/body/eval_jaxpr/cos | solution.py:29
  94.6 4.2 %fusion.52 = f32[512,64]{0,1:T(8,128)S(1)} fusion(f32[2048,64]{1,0:T(8,128)S(1)} %get-tuple-element.375, f32[512,1024]{1,0:T(8,128)S(1)} %get-tuple-element.334, f32[512,1024]{1,0:T(8,128)S(1)} %get-tuple-element.335), kind=kOutput, calls=%fused_computation.2.clone.1 | convolution fusion | flops 806354944 | bytes 4849664 | tf_op jit(solution)/shard_map/while/body/eval_jaxpr/dot_general | solution.py:37
  99.2 24.9 %all_gather.7 = f32[32,2,2048]{2,1,0:T(2,128)S(1)} all-gather(f32[1,2,2048]{2,1,0:T(2,128)S(1)} %bitcast.82), channel_id=1, replica_groups=mesh['pts'=16,'elem'=32] {'elem'}, dimensions={0}, use_global_device_ids=true | all-gather | bytes 540672 | tf_op jit(solution)/shard_map/all_gather | solution.py:14
  124.9 42.9 %while.25 = (s32[]{:T(128)}, f32[1024,64]{0,1:T(8,128)S(1)}, f32[4,512]{1,0:T(4,128)S(1)}, f32[4,512]{1,0:T(4,128)S(1)}, f32[4,512]{1,0:T(4,128)S(1)}, /*index=5...) while((s32[]{:T(128)}, f32[1024,64]{0,1:T(8,128)S(1)}, f32[4,512]{1,0:T(4,128)S(1)}, ...), condition=%wide.region_6.7_spmd.clone, body=%wide.region_5.6_spmd.clone.sunk | while | flops 807291904 | bytes 10780911 | solution.py:103
  125.3 7.3 %multiply_cosine_fusion.7 = (f32[512,1024]{1,0:T(8,128)S(1)}, f32[512,1024]{1,0:T(8,128)S(1)}) fusion(f32[1024]{0:T(1024)S(1)} %convert_add_fusion.6, f32[512]{0:T(512)S(1)} %bitcast.72), kind=kLoop, calls=%fused_computation.29.clone.1 | loop fusion | flops 524288 | bytes 4200448 | tf_op jit(solution)/shard_map/while/body/eval_jaxpr/cos | solution.py:59
  132.6 2.8 %fusion.58 = f32[2048,64]{0,1:T(8,128)S(1)} fusion(f32[512,1024]{1,0:T(8,128)S(1)} %get-tuple-element.347, f32[512,1024]{1,0:T(8,128)S(1)} %get-tuple-element.348, f32[512,32]{0,1:T(8,128)S(1)} %get-tuple-element.352, f32[512,32]{0,1:T(8,128)S(1)} %get-tuple-element.353), kind=kOutput, calls=%fused_computation.24.clone.1 | convolution fusion | flops 806387712 | bytes 4849664 | tf_op jit(solution)/shard_map/while/body/eval_jaxpr/dot_general | solution.py:61
  136.0 7.3 %multiply_cosine_fusion.7 = (f32[512,1024]{1,0:T(8,128)S(1)}, f32[512,1024]{1,0:T(8,128)S(1)}) fusion(f32[1024]{0:T(1024)S(1)} %convert_add_fusion.6, f32[512]{0:T(512)S(1)} %bitcast.72), kind=kLoop, calls=%fused_computation.29.clone.1 | loop fusion | flops 524288 | bytes 4200448 | tf_op jit(solution)/shard_map/while/body/eval_jaxpr/cos | solution.py:59
  143.3 2.8 %fusion.58 = f32[2048,64]{0,1:T(8,128)S(1)} fusion(f32[512,1024]{1,0:T(8,128)S(1)} %get-tuple-element.347, f32[512,1024]{1,0:T(8,128)S(1)} %get-tuple-element.348, f32[512,32]{0,1:T(8,128)S(1)} %get-tuple-element.352, f32[512,32]{0,1:T(8,128)S(1)} %get-tuple-element.353), kind=kOutput, calls=%fused_computation.24.clone.1 | convolution fusion | flops 806387712 | bytes 4849664 | tf_op jit(solution)/shard_map/while/body/eval_jaxpr/dot_general | solution.py:61
  146.7 7.3 %multiply_cosine_fusion.7 = (f32[512,1024]{1,0:T(8,128)S(1)}, f32[512,1024]{1,0:T(8,128)S(1)}) fusion(f32[1024]{0:T(1024)S(1)} %convert_add_fusion.6, f32[512]{0:T(512)S(1)} %bitcast.72), kind=kLoop, calls=%fused_computation.29.clone.1 | loop fusion | flops 524288 | bytes 4200448 | tf_op jit(solution)/shard_map/while/body/eval_jaxpr/cos | solution.py:59
  154.1 2.8 %fusion.58 = f32[2048,64]{0,1:T(8,128)S(1)} fusion(f32[512,1024]{1,0:T(8,128)S(1)} %get-tuple-element.347, f32[512,1024]{1,0:T(8,128)S(1)} %get-tuple-element.348, f32[512,32]{0,1:T(8,128)S(1)} %get-tuple-element.352, f32[512,32]{0,1:T(8,128)S(1)} %get-tuple-element.353), kind=kOutput, calls=%fused_computation.24.clone.1 | convolution fusion | flops 806387712 | bytes 4849664 | tf_op jit(solution)/shard_map/while/body/eval_jaxpr/dot_general | solution.py:61
  157.4 7.3 %multiply_cosine_fusion.7 = (f32[512,1024]{1,0:T(8,128)S(1)}, f32[512,1024]{1,0:T(8,128)S(1)}) fusion(f32[1024]{0:T(1024)S(1)} %convert_add_fusion.6, f32[512]{0:T(512)S(1)} %bitcast.72), kind=kLoop, calls=%fused_computation.29.clone.1 | loop fusion | flops 524288 | bytes 4200448 | tf_op jit(solution)/shard_map/while/body/eval_jaxpr/cos | solution.py:59
  164.8 2.8 %fusion.58 = f32[2048,64]{0,1:T(8,128)S(1)} fusion(f32[512,1024]{1,0:T(8,128)S(1)} %get-tuple-element.347, f32[512,1024]{1,0:T(8,128)S(1)} %get-tuple-element.348, f32[512,32]{0,1:T(8,128)S(1)} %get-tuple-element.352, f32[512,32]{0,1:T(8,128)S(1)} %get-tuple-element.353), kind=kOutput, calls=%fused_computation.24.clone.1 | convolution fusion | flops 806387712 | bytes 4849664 | tf_op jit(solution)/shard_map/while/body/eval_jaxpr/dot_general | solution.py:61
  167.8 1.0 copy.23
  168.8 64.5 %reduce-scatter.4.cloned.1.call-done = f32[64,64]{1,0:T(8,128)} async-done(((f32[1024,64]{1,0:T(8,128)}), f32[64,64]{1,0:T(8,128)}) %reduce-scatter.4.cloned.1.call-update) | async-done | bytes 16400 | tf_op jit(solution)/shard_map/reduce_scatter | solution.py:133
  233.3 0.9 fusion.34
  (72 shorter events, 6.3 us)
Async XLA Ops:
  7.2 226.2 %reduce-scatter.4.cloned.1.call-start = ((), (), s32[]{:S(2)}) async-start(), calls=%async_computation.1 | async-start | bytes 557056 | tf_op jit(solution)/shard_map/reduce_scatter | solution.py:133
  8.2 42.6 %copy-start.2 = (s32[2048]{0:T(1024)S(1)}, s32[2048]{0:T(1024)}, u32[]{:S(2)}) copy-start(s32[2048]{0:T(1024)} %param.13) | copy-start | bytes 24580
  8.3 42.6 %copy-start.3 = (s32[2048]{0:T(1024)S(1)}, s32[2048]{0:T(1024)}, u32[]{:S(2)}) copy-start(s32[2048]{0:T(1024)} %param.12) | copy-start | bytes 24580
  8.3 42.6 %copy-start.5 = (s32[32]{0:T(128)S(1)}, s32[32]{0:T(128)}, u32[]{:S(2)}) copy-start(s32[32]{0:T(128)} %param.11) | copy-start | bytes 388
  51.2 73.0 %copy-start.1 = (f32[2,2048]{1,0:T(2,128)S(1)}, f32[2,2048]{1,0:T(2,128)}, u32[]{:S(2)}) copy-start(f32[2,2048]{1,0:T(2,128)} %param.14) | copy-start | bytes 49156
  51.3 73.1 %copy-start.4 = (f32[2048]{0:T(1024)S(1)}, f32[2048]{0:T(1024)}, u32[]{:S(2)}) copy-start(f32[2048]{0:T(1024)} %param.15) | copy-start | bytes 24580
  124.3 0.6 copy-start
Sparse Core Ops, SparseCore 0:
  168.9 64.3 reduce-scatter.3
